TPU v7x, 1024 devices: a whole 8x8x8 slice. The times are simulated.
1024 devices in a mesh: blk: 16 (over x, y_lo), regroup: 16 (over z, core), hid: 4 (over y_hi).
Axes of the slice: x: 8, y: 8 (y_hi: 4, y_lo: 2; y = y_hi * 2 + y_lo), z: 8, core: 2. Of those that a mesh axis runs over, the one named last changes fastest.
Arguments:
- tokens: bfloat16 [4096, 6144], P(('blk', 'regroup')), may hold values from -6 to 6
- kinds: int32 [4096], P(('blk', 'regroup')), may hold values from 0 to 7
- slots: int32 [256, 16], P(('blk', 'regroup')), may hold values from 0 to 15, each once within a row
- gains: float32 [8, 6144], replicated, may hold values from 0.1 to 1.9
- gate_weight: bfloat16 [6144, 16384], P(None, ('blk', 'hid')), may hold values from -0.078125 to 0.078125
- up_weight: bfloat16 [6144, 16384], P(None, ('blk', 'hid')), may hold values from -0.078125 to 0.078125
- down_weight: bfloat16 [16384, 6144], P(('blk', 'hid')), may hold values from -0.125 to 0.125
Outputs:
- mixed: bfloat16 [4096, 6144], P(('blk', 'regroup'), 'hid')
Inputs may be any that keep to these rules, and one draw needn't show every extreme that they name: Each row of slots names every number 0 to 15 once.
All inputs are finite; a program needn't handle non-finite values.
Results may differ from a plain program's by a relative error of at most 0.019.
Values may be sent and summed in bfloat16 or wider, within the bound.
A program may use at most 64 MiB of HBM per device.

v0:
```python
import jax
import jax.numpy as jnp
from jax import lax
from jax.sharding import PartitionSpec as P

epsilon = 1e-05


def on_device(tokens, kinds, slots, gains, gate_weight, up_weight, down_weight):
    row_count = tokens.shape[0]
    feature_width = tokens.shape[1]
    lane_count = lax.axis_size("regroup")
    float_rows = tokens.astype(jnp.float32)
    row_scale = lax.rsqrt(jnp.mean(float_rows * float_rows, axis=1, keepdims=True) + epsilon)
    choose = (kinds[:, None] == jnp.arange(gains.shape[0], dtype=jnp.int32)[None, :]).astype(
        jnp.float32
    )
    row_gain = jnp.dot(choose, gains, precision=lax.Precision.HIGHEST)
    normed = (float_rows * row_scale * row_gain).astype(jnp.bfloat16)
    placing = (slots[0][None, :] == jnp.arange(row_count, dtype=jnp.int32)[:, None]).astype(
        jnp.bfloat16
    )
    ordered = jnp.dot(placing, normed, preferred_element_type=jnp.float32).astype(jnp.bfloat16)
    by_lane = ordered.reshape(row_count // lane_count, lane_count, feature_width)
    arranged = lax.all_to_all(by_lane, "regroup", split_axis=1, concat_axis=1, tiled=True).reshape(
        row_count, feature_width
    )
    panel = lax.all_gather(arranged, "blk", axis=0, tiled=True)
    gate_proj = jnp.dot(panel, gate_weight, preferred_element_type=jnp.float32)
    up_proj = jnp.dot(panel, up_weight, preferred_element_type=jnp.float32)
    hidden = (jax.nn.silu(gate_proj) * up_proj).astype(jnp.bfloat16)
    block_total = lax.psum_scatter(
        jnp.dot(hidden, down_weight, preferred_element_type=jnp.float32).astype(jnp.bfloat16),
        "blk",
        scatter_dimension=0,
        tiled=True,
    )
    summed = lax.psum_scatter(block_total, "hid", scatter_dimension=1, tiled=True).astype(
        jnp.float32
    )
    return summed.astype(jnp.bfloat16)


def solution(mesh):
    placed = (
        P(("blk", "regroup"), None),
        P(("blk", "regroup")),
        P(("blk", "regroup"), None),
        P(),
        P(None, ("blk", "hid")),
        P(None, ("blk", "hid")),
        P(("blk", "hid"), None),
    )
    return jax.shard_map(
        on_device,
        mesh=mesh,
        in_specs=placed,
        out_specs=P(("blk", "regroup"), "hid"),
        check_vma=False,
    )
```

profile of v0, /device:TPU:1, one launch (start us, length us, event | category | flops | bytes accessed | tf_op | source)
XLA Modules:
  0.0 265.7 jit_solution(2872362985873817336)
XLA Ops:
  6.5 0.0 copy-start
  6.5 0.0 all-gather.3.cloned.1.call-start
  6.5 1.2 fusion.14
  7.8 1.4 fusion
  9.2 0.8 fusion.1
  10.1 0.3 copy.12
  10.4 0.5 broadcast.24
  10.9 2.4 reduce
  13.3 1.1 reshape.18
  14.4 28.3 %all_to_all.5 = bf16[16,2,3072]{2,1,0:T(2,128)(2,1)} all-to-all(bf16[16,2,3072]{2,1,0:T(2,128)(2,1)S(1)} %reshape.18), channel_id=1, replica_groups=mesh['blk'=16,'regroup'=16,'hid'=4] {'regroup'}, dimensions={0} | all-to-all | bytes 393216 | tf_op jit(solution)/shard_map/all_to_all | solution.py:25
  42.7 1.6 reshape.19
  44.2 0.8 copy.10
  45.0 0.0 all-gather.3.cloned.1.call-update
  45.1 0.0 reduce-scatter.3.cloned.1.call-start
  45.1 78.3 %all-gather.3.cloned.1.call-done = bf16[1,256,6144]{2,1,0:T(8,128)(2,1)} async-done(((bf16[1,16,6144]{2,1,0:T(8,128)(2,1)}), bf16[1,256,6144]{2,1,0:T(8,128)(2,1)}) %all-gather.3.cloned.1.call-update) | async-done | bytes 3145744 | tf_op jit(solution)/shard_map/all_gather | solution.py:28
  123.4 3.8 %fusion.4 = f32[256,256]{1,0:T(8,128)S(1)} fusion(bf16[6144,256]{1,0:T(8,128)(2,1)} %param.11, bf16[1,256,6144]{2,1,0:T(8,128)(2,1)} %all-gather.3.cloned.1.call-done), kind=kOutput, calls=%fused_computation.7 | convolution fusion | flops 805306368 | bytes 6553600 | tf_op jit(solution)/shard_map/dot_general | solution.py:29
  127.2 0.0 copy-done
  127.3 8.0 %convolution_convert_fusion = bf16[256,6144]{1,0:T(8,128)(2,1)} fusion(bf16[256,6144]{1,0:T(8,128)(2,1)S(1)} %copy-done, bf16[6144,256]{1,0:T(8,128)(2,1)} %param.12, bf16[1,256,6144]{2,1,0:T(8,128)(2,1)} %all-gather.3.cloned.1.call-done, f32[256,256]{1,0:T(8,128)S(1)} %fusion.4), kind=kOutput, calls=%fused_computation | convolution fusion | flops 1612578816 | bytes 12845056 | tf_op jit(solution)/shard_map/dot_general | solution.py:33
  135.3 0.0 reduce-scatter.3.cloned.1.call-update
  135.3 0.0 reduce-scatter.5.cloned.1.call-start
  135.3 86.1 %reduce-scatter.3.cloned.1.call-done = bf16[16,6144]{1,0:T(8,128)(2,1)} async-done(((bf16[256,6144]{1,0:T(8,128)(2,1)}), bf16[16,6144]{1,0:T(8,128)(2,1)}) %reduce-scatter.3.cloned.1.call-update) | async-done | bytes 196624 | tf_op jit(solution)/shard_map/reduce_scatter | solution.py:32
  221.4 0.0 reduce-scatter.5.cloned.1.call-update
  221.4 37.7 %reduce-scatter.5.cloned.1.call-done = bf16[16,1536]{1,0:T(8,128)(2,1)} async-done(((bf16[16,6144]{1,0:T(8,128)(2,1)}), bf16[16,1536]{1,0:T(8,128)(2,1)}) %reduce-scatter.5.cloned.1.call-update) | async-done | bytes 49168 | tf_op jit(solution)/shard_map/reduce_scatter | solution.py:38
  (1 shorter events, 0.0 us)
Async XLA Ops:
  6.5 120.7 %copy-start = (bf16[256,6144]{1,0:T(8,128)(2,1)S(1)}, bf16[256,6144]{1,0:T(8,128)(2,1)}, u32[]{:S(2)}) copy-start(bf16[256,6144]{1,0:T(8,128)(2,1)} %param.13) | copy-start | bytes 9437188
  6.5 116.9 %all-gather.3.cloned.1.call-start = ((), (), s32[]{:S(2)}) async-start(), calls=%async_computation.5 | async-start | bytes 3342336 | tf_op jit(solution)/shard_map/all_gather | solution.py:28
  45.1 176.3 %reduce-scatter.3.cloned.1.call-start = ((), (), s32[]{:S(2)}) async-start(), calls=%async_computation.3 | async-start | bytes 3342336 | tf_op jit(solution)/shard_map/reduce_scatter | solution.py:32
  135.3 123.9 %reduce-scatter.5.cloned.1.call-start = ((), (), s32[]{:S(2)}) async-start(), calls=%async_computation.4 | async-start | bytes 245760 | tf_op jit(solution)/shard_map/reduce_scatter | solution.py:38
Sparse Core Ops, SparseCore 0:
  45.2 78.1 all-gather.2
  135.4 85.9 reduce-scatter.2
  224.8 34.3 reduce-scatter.4
where the time goes:
time: 267 us; the launch traced here: 266 us
  waiting for transfers between devices  202 us (76%)
  blocking collectives  28.3 us (11%)
  matrix products  14.1 us (5%)
  between operations  13.2 us (5%)
  local copies, waits for them, and re-layouts  4.26 us (2%)
  other arithmetic  3.67 us (1%)
    reduce_scatter x1, waiting for transfers between devices, on_device(): lax.psum_scatter(jnp.dot(hidden, down_weight, preferred_element_type=jnp....  86.1 us
    all_gather x1, waiting for transfers between devices, on_device(): panel = lax.all_gather(arranged, 'blk', axis=0, tiled=True)  78.3 us
    reduce_scatter x1, waiting for transfers between devices, on_device(): lax.psum_scatter(block_total, 'hid', scatter_dimension=1, tiled=True)  37.7 us
    all_to_all x1, blocking collectives, on_device(): lax.all_to_all(by_lane, 'regroup', split_axis=1, concat_axis=1, tiled=True)  28.3 us
    dot_general x1, matrix products, on_device(): jnp.dot(hidden, down_weight, preferred_element_type=jnp.float32)  8.01 us
  transfers between devices with their start and end apart: 3, of which 3 were waited for; matrix products, arithmetic and copies ran while one was open for 0% of the time, Pallas kernels for 0%

commit v1 on v0

v1 whole, which is shorter than its diff:
```python
import jax
import jax.numpy as jnp
from jax import lax
from jax.experimental import pallas as pl
from jax.experimental.pallas import tpu as pltpu
from jax.sharding import PartitionSpec as P

MESH = pl.DeviceIdType.MESH
epsilon = 1e-05
D = 6144
HALF = D // 2
EIGHTH = D // 8
UNITS = 256
SLOT = {0: 0, 1: 1, 7: 2, 2: 3, 6: 4, 3: 5, 5: 6, 4: 7}
AHEAD = {u: d for d, u in SLOT.items()}
KSTEP = 1536


def kernel(
    tokens_ref, kinds_ref, slots_ref, gains_ref, gate_hbm, up_hbm, down_hbm, out_ref,
    panel, wg, wu, wd, hid, acc_g, acc_u, part_f, part, arrived, outgo, final, rows,
    load_sem, xs, xr, ys, yr, ws, wr, zs, zr, cs, cr, hs, hr, ps, pr, fs, fr, own_sem,
):
    blk, reg, hidx = lax.axis_index("blk"), lax.axis_index("regroup"), lax.axis_index("hid")
    x, ylo = lax.div(blk, 2), lax.rem(blk, 2)
    y = hidx * 2 + ylo
    z, core = lax.div(reg, 2), lax.rem(reg, 2)

    def device(x_at, y_at, reg_at):
        return (x_at * 2 + lax.rem(y_at, 2), reg_at, lax.div(y_at, 2))

    def along_x(d):
        return device(lax.rem(x + d, 8), y, reg)

    def along_y(d):
        return device(x, lax.rem(y + d, 8), reg)

    def along_z(d):
        return device(x, y, lax.rem(z + d, 8) * 2 + core)

    partner = device(x, y, z * 2 + 1 - core)
    y_other = hidx * 2 + 1 - ylo

    def regroup_peer(swap, t):
        return device(x, y_other if swap else y, lax.rem(reg + t, 16))

    barrier = pltpu.get_barrier_semaphore()
    peers = [along_x(d) for d in range(1, 8)] + [along_y(d) for d in range(1, 8)]
    peers += [regroup_peer(swap, t) for swap in (0, 1) for t in range(1, 16)]
    for peer in peers:
        pl.semaphore_signal(barrier, inc=1, device_id=peer, device_id_type=MESH)

    loads = [
        pltpu.make_async_copy(gate_hbm, wg, load_sem.at[0]),
        pltpu.make_async_copy(up_hbm, wu, load_sem.at[1]),
        pltpu.make_async_copy(
            down_hbm.at[:, pl.ds(pl.multiple_of(y * EIGHTH, 128), EIGHTH)], wd.at[0], load_sem.at[2]
        ),
    ]
    for load in loads:
        load.start()

    slot_row = slots_ref[...]
    here = lax.broadcasted_iota(jnp.int32, (16, 16), 0) == jnp.broadcast_to(slot_row, (16, 16))
    placing = jnp.where(here, 1.0, 0.0).astype(jnp.bfloat16)
    kind = jnp.sum(
        jnp.where(here, jnp.broadcast_to(kinds_ref[...], (16, 16)).astype(jnp.float32), 0.0),
        axis=1, keepdims=True,
    )
    values = jnp.dot(placing, tokens_ref[...], preferred_element_type=jnp.float32)
    scale = lax.rsqrt(jnp.mean(values * values, axis=1, keepdims=True) + epsilon)
    gain = jnp.broadcast_to(gains_ref[0:1, :], (16, D))
    for k in range(1, 8):
        gain = jnp.where(kind == float(k), jnp.broadcast_to(gains_ref[k : k + 1, :], (16, D)), gain)
    panel[ylo, 0] = (values * scale * gain).astype(jnp.bfloat16)

    pl.semaphore_wait(barrier, len(peers))
    sends = []

    def push(source, target, send_sem, recv_sem, peer):
        copy = pltpu.make_async_remote_copy(
            src_ref=source, dst_ref=target, send_sem=send_sem, recv_sem=recv_sem,
            device_id=peer, device_id_type=MESH,
        )
        copy.start()
        sends.append(copy)

    def arrive(target, send_sem, recv_sem):
        pltpu.make_async_remote_copy(
            src_ref=target, dst_ref=target, send_sem=send_sem, recv_sem=recv_sem,
            device_id=partner, device_id_type=MESH,
        ).wait_recv()

    def half(lane, d, h):
        return panel.at[lane, SLOT[d % 8], :, pl.ds(h * HALF, HALF)]

    def x_send(step, direction, h):
        d = (-step if direction == 0 else step) % 8
        to = (d - 1 if direction == 0 else d + 1) % 8
        push(half(ylo, d, h), half(ylo, to, h), xs.at[direction, step, h], xr.at[direction, step, h],
             along_x(1 if direction == 0 else 7))

    def x_wait(step, direction, h):
        d = (-step - 1 if direction == 0 else step + 1) % 8
        arrive(half(ylo, d, h), xs.at[direction, step, h], xr.at[direction, step, h])

    def y_send(d, h):
        push(half(ylo, d, h), half(ylo, d, h), ys.at[SLOT[d], h], yr.at[SLOT[d], h],
             along_y(1 if h == 0 else 7))

    def y_wait(u):
        for h in (0, 1):
            arrive(half(1 - ylo, AHEAD[u], h), ys.at[u, h], yr.at[u, h])

    def x_step(step):
        if step < 3:
            for h in (0, 1):
                for direction in (0, 1):
                    x_wait(step, direction, h)
                    if step < 2 or h == direction:
                        x_send(step + 1, direction, h)
                for direction in (0, 1):
                    y_send((-step - 1 if direction == 0 else step + 1) % 8, h)
        else:
            for h in (0, 1):
                x_wait(3, h, h)
                y_send(4, h)

    def piece(q, lo=0, width=EIGHTH):
        return wd.at[pl.ds(1, 7), pl.ds(pl.multiple_of(q * 16, 16), 16), pl.ds(lo, width)]

    def z_at(d):
        return lax.rem(z + d + 8, 8) * 2 + core

    def z_send(step, direction):
        q = z_at(-step if direction == 0 else step)
        lo, width = (0, EIGHTH) if step < 3 else (direction * (EIGHTH // 2), EIGHTH // 2)
        push(piece(q, lo, width), piece(q, lo, width), zs.at[direction, step], zr.at[direction, step],
             along_z(1 if direction == 0 else 7))

    def core_send(d):
        push(piece(z_at(d)), piece(z_at(d)), cs.at[d % 8], cr.at[d % 8], partner)

    def z_step(step):
        for direction in (0, 1):
            q = z_at(-step - 1 if direction == 0 else step + 1)
            lo, width = (0, EIGHTH) if step < 3 else (direction * (EIGHTH // 2), EIGHTH // 2)
            arrive(piece(q, lo, width), zs.at[direction, step], zr.at[direction, step])
            if step < 3:
                z_send(step + 1, direction)
                core_send(-step - 1 if direction == 0 else step + 1)
        if step == 3:
            core_send(4)

    def core_wait():
        for d in range(8):
            q = lax.rem(z + d, 8) * 2 + 1 - core
            arrive(piece(q), cs.at[d], cr.at[d])

    def hidden_at(dy, group, lo=0, count=128):
        return hid.at[dy % 8, group, pl.ds(lo, count), :]

    def hidden_send(group, step, direction):
        dy = -step if direction == 0 else step
        lo, count = (0, 128) if step < 3 else (direction * 64, 64)
        push(hidden_at(dy, group, lo, count),
             hidden_at(dy - 1 if direction == 0 else dy + 1, group, lo, count),
             hs.at[group, direction, step], hr.at[group, direction, step],
             along_y(1 if direction == 0 else 7))

    def hidden_step(group, step):
        for direction in (0, 1):
            dy = -step - 1 if direction == 0 else step + 1
            lo, count = (0, 128) if step < 3 else (direction * 64, 64)
            arrive(hidden_at(dy, group, lo, count), hs.at[group, direction, step],
                   hr.at[group, direction, step])
            if step < 3:
                hidden_send(group, step + 1, direction)

    def gate_up(group):
        acc_g[...] = jnp.zeros_like(acc_g)
        acc_u[...] = jnp.zeros_like(acc_u)

        def one(k, carry):
            span = pl.ds(pl.multiple_of(k * KSTEP, KSTEP), KSTEP)
            block = panel[:, 4 * group : 4 * group + 4, :, span].reshape(128, KSTEP)
            acc_g[...] += jnp.dot(block, wg[span, :], preferred_element_type=jnp.float32)
            acc_u[...] += jnp.dot(block, wu[span, :], preferred_element_type=jnp.float32)
            return carry

        lax.fori_loop(0, D // KSTEP, one, 0)
        v = acc_g[...]
        hid[0, group] = (v / (1.0 + jnp.exp(-v)) * acc_u[...]).astype(jnp.bfloat16)
        for direction in (0, 1):
            hidden_send(group, 0, direction)

    def down(group, pieces, first):
        for dy in pieces:
            term = jnp.dot(hid[dy, group], wd[dy], preferred_element_type=jnp.float32)
            if first and dy == pieces[0]:
                part_f[group] = term
            else:
                part_f[group] += term

    def part_send(group):
        part[:, 4 * group : 4 * group + 4] = part_f[group].reshape(2, 4, 16, EIGHTH).astype(jnp.bfloat16)
        for u in reversed(range(4 * group, 4 * group + 4)):
            d = AHEAD[u]
            if d:
                push(part.at[:, u], arrived.at[d], ps.at[d], pr.at[d], along_x(d))

    for h in (0, 1):
        for direction in (0, 1):
            x_send(0, direction, h)
        y_send(0, h)
    for t in (4, 3, 5, 2, 6, 1, 7):
        y_to = lax.rem(y + t, 8)
        push(
            down_hbm.at[pl.ds(pl.multiple_of(reg * 16, 16), 16),
                        pl.ds(pl.multiple_of(y_to * EIGHTH, 128), EIGHTH)],
            wd.at[8 - t, pl.ds(pl.multiple_of(reg * 16, 16), 16), :],
            ws.at[8 - t], wr.at[8 - t], along_y(t),
        )
    x_step(0)
    x_step(1)
    for t in range(1, 8):
        arrive(wd.at[t, pl.ds(pl.multiple_of(reg * 16, 16), 16), :], ws.at[t], wr.at[t])
    z_send(0, 0)
    z_send(0, 1)
    core_send(0)
    x_step(2)
    z_step(0)
    loads[0].wait()
    loads[1].wait()
    for u in range(4):
        y_wait(u)
    gate_up(0)
    x_step(3)
    z_step(1)
    hidden_step(0, 0)
    for u in range(4, 8):
        y_wait(u)
    gate_up(1)
    z_step(2)
    hidden_step(0, 1)
    hidden_step(0, 2)
    z_step(3)
    hidden_step(1, 0)
    hidden_step(0, 3)
    loads[2].wait()
    core_wait()
    down(0, range(8), True)
    part_send(0)
    hidden_step(1, 1)
    down(1, (0, 1, 7), True)
    hidden_step(1, 2)
    down(1, (2, 6), False)
    hidden_step(1, 3)
    down(1, (3, 5, 4), False)
    part_send(1)

    for lane in (0, 1):
        rows[lane] = part_f[0, 64 * lane : 64 * lane + 16, :]
    for d in (1, 7, 2, 6, 3, 5, 4):
        arrive(arrived.at[d], ps.at[d], pr.at[d])
        rows[...] += arrived[d].astype(jnp.float32)
    for lane in (0, 1):
        for j in range(16):
            outgo[lane, j] = rows[lane, j : j + 1, :]
    own = pltpu.make_async_copy(outgo.at[ylo, reg], final.at[ylo, reg], own_sem)
    own.start()
    for swap in (0, 1):
        lane = 1 - ylo if swap else ylo
        for t in range(16):
            if swap or t:
                push(outgo.at[lane, lax.rem(reg + t, 16)], final.at[ylo, reg],
                     fs.at[swap, t], fr.at[swap, t], regroup_peer(swap, t))
    own.wait()
    for swap in (0, 1):
        lane = 1 - ylo if swap else ylo
        for t in range(16):
            if swap or t:
                arrive(final.at[lane, lax.rem(reg + 16 - t, 16)], fs.at[swap, t], fr.at[swap, t])
    for lane in (0, 1):
        for g in range(16):
            rows[lane, g : g + 1, :] = final[lane, g]
        out_ref[:, lane * EIGHTH : (lane + 1) * EIGHTH] = rows[lane].astype(jnp.bfloat16)
    for copy in sends:
        copy.wait_send()


def on_device(tokens, kinds, slots, gains, gate_weight, up_weight, down_weight):
    vmem = pl.BlockSpec(memory_space=pltpu.VMEM)
    hbm = pl.BlockSpec(memory_space=pl.ANY)
    bf16, f32, dma = jnp.bfloat16, jnp.float32, pltpu.SemaphoreType.DMA
    return pl.pallas_call(
        kernel,
        out_shape=jax.ShapeDtypeStruct((16, D // 4), bf16),
        in_specs=[vmem, vmem, vmem, vmem, hbm, hbm, hbm],
        out_specs=vmem,
        scratch_shapes=[
            pltpu.VMEM((2, 8, 16, D), bf16),
            pltpu.VMEM((D, UNITS), bf16),
            pltpu.VMEM((D, UNITS), bf16),
            pltpu.VMEM((8, UNITS, EIGHTH), bf16),
            pltpu.VMEM((8, 2, 128, UNITS), bf16),
            pltpu.VMEM((128, UNITS), f32),
            pltpu.VMEM((128, UNITS), f32),
            pltpu.VMEM((2, 128, EIGHTH), f32),
            pltpu.VMEM((2, 8, 16, EIGHTH), bf16),
            pltpu.VMEM((8, 2, 16, EIGHTH), bf16),
            pltpu.VMEM((2, 16, 1, EIGHTH), f32),
            pltpu.VMEM((2, 16, 1, EIGHTH), f32),
            pltpu.VMEM((2, 16, EIGHTH), f32),
            dma((3,)),
            dma((2, 4, 2)), dma((2, 4, 2)),
            dma((8, 2)), dma((8, 2)),
            dma((8,)), dma((8,)),
            dma((2, 4)), dma((2, 4)),
            dma((8,)), dma((8,)),
            dma((2, 2, 4)), dma((2, 2, 4)),
            dma((8,)), dma((8,)),
            dma((2, 16)), dma((2, 16)),
            dma(()),
        ],
        compiler_params=pltpu.CompilerParams(collective_id=0, has_side_effects=True),
    )(tokens, kinds.reshape(1, 16), slots, gains, gate_weight, up_weight, down_weight)


def solution(mesh):
    placed = (
        P(("blk", "regroup"), None),
        P(("blk", "regroup")),
        P(("blk", "regroup"), None),
        P(),
        P(None, ("blk", "hid")),
        P(None, ("blk", "hid")),
        P(("blk", "hid"), None),
    )
    return jax.shard_map(
        on_device,
        mesh=mesh,
        in_specs=placed,
        out_specs=P(("blk", "regroup"), "hid"),
        check_vma=False,
    )
```

time: 267 us -> 85.5 us (0.32)
  waiting for transfers between devices: 202 us -> 0 us
  Pallas kernels: 0 us -> 83.8 us
  blocking collectives: 28.3 us -> 0 us
  matrix products: 14.1 us -> 0 us
  between operations: 13.2 us -> 0.01 us
  other arithmetic: 3.67 us -> 0 us
  local copies, waits for them, and re-layouts: 4.26 us -> 1.42 us
    reduce_scatter x2 -> x0, waiting for transfers between devices: 124 us -> none  [the longest x1 86.1 us: on_device(): lax.psum_scatter(jnp.dot(hidden, down_weight, preferred_element_type=jnp....]
    pallas_call x0 -> x1, Pallas kernels: none -> 83.8 us  [on_device(): pl.pallas_call(kernel, out_shape=jax.ShapeDtypeStruct((16, D // 4), bf16)...]
    all_gather x1 -> x0, waiting for transfers between devices: 78.3 us -> none  [on_device(): panel = lax.all_gather(arranged, 'blk', axis=0, tiled=True)]
    all_to_all x1 -> x0, blocking collectives: 28.3 us -> none  [on_device(): lax.all_to_all(by_lane, 'regroup', split_axis=1, concat_axis=1, tiled=True)]
    dot_general x4 -> x0, matrix products: 14.1 us -> none  [the longest x1 8.01 us: on_device(): jnp.dot(hidden, down_weight, preferred_element_type=jnp.float32)]
  transfers between devices with their start and end apart: 3 -> 0, of which waited for: 3 -> 0; matrix products, arithmetic and copies ran while one was open for 0% -> 0% of each run, Pallas kernels for 0% -> 0%
where the time goes in v1:
time: 85.5 us; the launch traced here: 85.3 us
  Pallas kernels  83.8 us (98%)
  local copies, waits for them, and re-layouts  1.42 us (2%)
    pallas_call x1, Pallas kernels, on_device(): pl.pallas_call(kernel, out_shape=jax.ShapeDtypeStruct((16, D // 4), bf16)...  83.8 us

profile of v1, /device:TPU:1, one launch (start us, length us, event | category | flops | bytes accessed | tf_op | source)
XLA Modules:
  0.0 85.3 jit_solution(12836370006404802864)
XLA Ops:
  0.0 83.8 %shard_map.73 = bf16[16,1536]{1,0:T(8,128)(2,1)} custom-call(bf16[16,6144]{1,0:T(8,128)(2,1)} %tokens_ref.1, s32[1,16]{1,0:T(1,128)} %bitcast.1, s32[1,16]{1,0:T(1,128)} %slots_ref.1, f32[8,6144]{1,0:T(8,128)} %gains_ref.1, bf16[6144,256]{1,0:T(8,128)(2,1)} %gate_hbm.1, bf16[6144,256]{1,0:T(8,128)(2,1)} %up_hbm.1, bf16[256,6144]{1,0:T(8,128)(2,1)} %down_hbm.1), custom_call_target="tpu_custom_call" | custom-call | tf_op jit(solution)/shard_map/pallas_call | solution.py:296
  83.8 1.4 %copy.9 = bf16[16,1536]{1,0:T(8,128)(2,1)} copy(bf16[16,1536]{1,0:T(8,128)(2,1)} %shard_map.73) | data formatting | bytes 98304

commit v2 on v1

v2 whole, which is shorter than its diff:
```python
import jax
import jax.numpy as jnp
from jax import lax
from jax.experimental import pallas as pl
from jax.experimental.pallas import tpu as pltpu
from jax.sharding import PartitionSpec as P

MESH = pl.DeviceIdType.MESH
epsilon = 1e-05
D = 6144
HALF = D // 2
EIGHTH = D // 8
UNITS = 256
SLOT = {0: 0, 1: 1, 7: 2, 2: 3, 6: 4, 3: 5, 5: 6, 4: 7}
AHEAD = {u: d for d, u in SLOT.items()}
KSTEP = 1536
MID, MID_WIDTH = 2304, 1536
GROUPS = ((0, 4), (4, 6), (6, 8))


def rows_of(group):
    lo, hi = GROUPS[group]
    return 32 * lo, 32 * (hi - lo)


def kernel(
    tokens_hbm, kinds_hbm, slots_hbm, gains_hbm, gate_hbm, up_hbm, down_hbm, out_ref,
    tokens_ref, kinds_ref, slots_ref, gains_ref, panel, wg, wu, wd, hid, acc_g, acc_u, part_f, part, arrived, outgo, final, rows,
    load_sem, xs, xr, ms, mr, ys, yr, ws, wr, zs, zr, cs, cr, hs, hr, ps, pr, fs, fr, own_sem,
):
    blk, reg, hidx = lax.axis_index("blk"), lax.axis_index("regroup"), lax.axis_index("hid")
    x, ylo = lax.div(blk, 2), lax.rem(blk, 2)
    y = hidx * 2 + ylo
    z, core = lax.div(reg, 2), lax.rem(reg, 2)

    def device(x_at, y_at, reg_at):
        return (x_at * 2 + lax.rem(y_at, 2), reg_at, lax.div(y_at, 2))

    def along_x(d):
        return device(lax.rem(x + d, 8), y, reg)

    def along_y(d):
        return device(x, lax.rem(y + d, 8), reg)

    def along_z(d):
        return device(x, y, lax.rem(z + d, 8) * 2 + core)

    partner = device(x, y, z * 2 + 1 - core)
    y_other = hidx * 2 + 1 - ylo

    def regroup_peer(swap, t):
        return device(x, y_other if swap else y, lax.rem(reg + t, 16))

    inputs = [
        pltpu.make_async_copy(tokens_hbm, tokens_ref, load_sem.at[3]),
        pltpu.make_async_copy(gains_hbm, gains_ref, load_sem.at[4]),
        pltpu.make_async_copy(kinds_hbm, kinds_ref, load_sem.at[5]),
        pltpu.make_async_copy(slots_hbm, slots_ref, load_sem.at[6]),
    ]
    for copy in inputs:
        copy.start()

    barrier = pltpu.get_barrier_semaphore()
    peers = [along_y(d) for d in (4, 3, 5, 2, 6, 1, 7)] + [along_x(1), along_x(7)]
    peers += [along_z(1), along_z(7), partner]
    for peer in peers:
        pl.semaphore_signal(barrier, inc=1, device_id=peer, device_id_type=MESH)

    loads = [
        pltpu.make_async_copy(gate_hbm, wg, load_sem.at[0]),
        pltpu.make_async_copy(up_hbm, wu, load_sem.at[1]),
        pltpu.make_async_copy(
            down_hbm.at[:, pl.ds(pl.multiple_of(y * EIGHTH, 128), EIGHTH)], wd.at[0], load_sem.at[2]
        ),
    ]
    for load in loads:
        load.start()
    for copy in inputs:
        copy.wait()

    slot_row = slots_ref[...]
    here = lax.broadcasted_iota(jnp.int32, (16, 16), 0) == jnp.broadcast_to(slot_row, (16, 16))
    placing = jnp.where(here, 1.0, 0.0).astype(jnp.bfloat16)
    kind = jnp.sum(
        jnp.where(here, jnp.broadcast_to(kinds_ref[...], (16, 16)).astype(jnp.float32), 0.0),
        axis=1, keepdims=True,
    )
    values = jnp.dot(placing, tokens_ref[...], preferred_element_type=jnp.float32)
    scale = lax.rsqrt(jnp.mean(values * values, axis=1, keepdims=True) + epsilon)
    gain = jnp.broadcast_to(gains_ref[0:1, :], (16, D))
    for k in range(1, 8):
        gain = jnp.where(kind == float(k), jnp.broadcast_to(gains_ref[k : k + 1, :], (16, D)), gain)
    panel[ylo, 0] = (values * scale * gain).astype(jnp.bfloat16)

    pl.semaphore_wait(barrier, len(peers))
    sends = []

    def push(source, target, send_sem, recv_sem, peer):
        copy = pltpu.make_async_remote_copy(
            src_ref=source, dst_ref=target, send_sem=send_sem, recv_sem=recv_sem,
            device_id=peer, device_id_type=MESH,
        )
        copy.start()
        sends.append(copy)

    def arrive(target, send_sem, recv_sem):
        pltpu.make_async_remote_copy(
            src_ref=target, dst_ref=target, send_sem=send_sem, recv_sem=recv_sem,
            device_id=partner, device_id_type=MESH,
        ).wait_recv()

    def half(lane, d, h):
        return panel.at[lane, SLOT[d % 8], :, pl.ds(h * HALF, HALF)]

    def x_send(step, direction, h):
        d = (-step if direction == 0 else step) % 8
        to = (d - 1 if direction == 0 else d + 1) % 8
        push(half(ylo, d, h), half(ylo, to, h), xs.at[direction, step, h], xr.at[direction, step, h],
             along_x(1 if direction == 0 else 7))

    def x_wait(step, direction, h):
        d = (-step - 1 if direction == 0 else step + 1) % 8
        arrive(half(ylo, d, h), xs.at[direction, step, h], xr.at[direction, step, h])

    def y_part(lane, d, h):
        if d == 0:
            return half(lane, d, h)
        lo, width = (0, MID) if h == 0 else (MID + MID_WIDTH, D - MID - MID_WIDTH)
        return panel.at[lane, SLOT[d], :, pl.ds(lo, width)]

    def y_send(d, h):
        push(y_part(ylo, d, h), y_part(ylo, d, h), ys.at[SLOT[d], h], yr.at[SLOT[d], h],
             along_y(1 if h == 0 else 7))

    def y_wait(u):
        for h in (0, 1):
            arrive(y_part(1 - ylo, AHEAD[u], h), ys.at[u, h], yr.at[u, h])

    def mid(d, step, direction):
        lo, width = (MID, MID_WIDTH) if step < 3 else (MID + direction * (MID_WIDTH // 2), MID_WIDTH // 2)
        return panel.at[1 - ylo, SLOT[d % 8], :, pl.ds(lo, width)]

    def mid_send(step, direction):
        d = -step if direction == 0 else step
        to = d - 1 if direction == 0 else d + 1
        push(mid(d, step, direction), mid(to, step, direction), ms.at[direction, step],
             mr.at[direction, step], along_x(1 if direction == 0 else 7))

    def mid_step(step):
        for direction in (0, 1):
            d = -step - 1 if direction == 0 else step + 1
            arrive(mid(d, step, direction), ms.at[direction, step], mr.at[direction, step])
            if step < 3:
                mid_send(step + 1, direction)

    def x_step(step, h):
        if step < 3:
            for direction in (0, 1):
                x_wait(step, direction, h)
                if step < 2 or h == direction:
                    x_send(step + 1, direction, h)
            for direction in (0, 1):
                y_send((-step - 1 if direction == 0 else step + 1) % 8, h)
        else:
            x_wait(3, h, h)
            y_send(4, h)

    def piece(q, part):
        return wd.at[pl.ds(1, 7), pl.ds(pl.multiple_of(q * 16, 16), 16), pl.ds(part * (EIGHTH // 2), EIGHTH // 2)]

    def z_at(d):
        return lax.rem(z + d + 8, 8) * 2 + core

    def z_send(step, direction, part):
        q = z_at(-step if direction == 0 else step)
        push(piece(q, part), piece(q, part), zs.at[direction, step, part], zr.at[direction, step, part],
             along_z(1 if direction == 0 else 7))

    def core_send(d, part):
        push(piece(z_at(d), part), piece(z_at(d), part), cs.at[d % 8, part], cr.at[d % 8, part], partner)

    def z_start():
        for part in (0, 1):
            for direction in (0, 1):
                z_send(0, direction, part)
        for part in (0, 1):
            core_send(0, part)

    def z_step(step, part):
        for direction in (0, 1) if step < 3 else (part,):
            d = -step - 1 if direction == 0 else step + 1
            arrive(piece(z_at(d), part), zs.at[direction, step, part], zr.at[direction, step, part])
            if step < 2 or (step == 2 and direction == part):
                z_send(step + 1, direction, part)
            core_send(4 if step == 3 else d, part)

    def core_wait():
        for d in range(8):
            q = lax.rem(z + d, 8) * 2 + 1 - core
            for part in (0, 1):
                arrive(piece(q, part), cs.at[d, part], cr.at[d, part])

    def hidden_at(dy, group, step, direction):
        start, count = rows_of(group)
        if step == 3:
            start, count = start + direction * (count // 2), count // 2
        return hid.at[dy % 8, pl.ds(start, count), :]

    def hidden_send(group, step, direction):
        dy = -step if direction == 0 else step
        push(hidden_at(dy, group, step, direction),
             hidden_at(dy - 1 if direction == 0 else dy + 1, group, step, direction),
             hs.at[group, direction, step], hr.at[group, direction, step],
             along_y(1 if direction == 0 else 7))

    def hidden_step(group, step):
        for direction in (0, 1):
            dy = -step - 1 if direction == 0 else step + 1
            arrive(hidden_at(dy, group, step, direction), hs.at[group, direction, step],
                   hr.at[group, direction, step])
            if step < 3:
                hidden_send(group, step + 1, direction)

    def gate_up(group):
        (lo, hi), (start, count) = GROUPS[group], rows_of(group)
        acc_g[0:count, :] = jnp.zeros((count, UNITS), jnp.float32)
        acc_u[0:count, :] = jnp.zeros((count, UNITS), jnp.float32)

        def one(k, carry):
            span = pl.ds(pl.multiple_of(k * KSTEP, KSTEP), KSTEP)
            block = panel[:, lo:hi, :, span].reshape(count, KSTEP)
            acc_g[0:count, :] += jnp.dot(block, wg[span, :], preferred_element_type=jnp.float32)
            acc_u[0:count, :] += jnp.dot(block, wu[span, :], preferred_element_type=jnp.float32)
            return carry

        lax.fori_loop(0, D // KSTEP, one, 0)
        v = acc_g[0:count, :]
        hid[0, start : start + count, :] = (v / (1.0 + jnp.exp(-v)) * acc_u[0:count, :]).astype(jnp.bfloat16)
        for direction in (0, 1):
            hidden_send(group, 0, direction)

    def down(group, pieces, first):
        start, count = rows_of(group)
        for dy in pieces:
            term = jnp.dot(hid[dy, start : start + count, :], wd[dy], preferred_element_type=jnp.float32)
            if first and dy == pieces[0]:
                part_f[start : start + count, :] = term
            else:
                part_f[start : start + count, :] += term

    def part_send(group):
        (lo, hi), (start, count) = GROUPS[group], rows_of(group)
        part[:, lo:hi] = part_f[start : start + count, :].reshape(2, hi - lo, 16, EIGHTH).astype(jnp.bfloat16)
        for u in reversed(range(lo, hi)):
            d = AHEAD[u]
            if d:
                push(part.at[:, u], arrived.at[d], ps.at[d], pr.at[d], along_x(d))

    def weights_wait():
        for t in range(1, 8):
            arrive(wd.at[t, pl.ds(pl.multiple_of(reg * 16, 16), 16), :], ws.at[t], wr.at[t])

    def y_waits(lo, hi):
        for u in range(lo, hi):
            y_wait(u)

    for h in (0, 1):
        for direction in (0, 1):
            x_send(0, direction, h)
        y_send(0, h)
    for t in (4, 3, 5, 2, 6, 1, 7):
        y_to = lax.rem(y + t, 8)
        push(
            down_hbm.at[pl.ds(pl.multiple_of(reg * 16, 16), 16),
                        pl.ds(pl.multiple_of(y_to * EIGHTH, 128), EIGHTH)],
            wd.at[8 - t, pl.ds(pl.multiple_of(reg * 16, 16), 16), :],
            ws.at[8 - t], wr.at[8 - t], along_y(t),
        )
    x_step(0, 0)
    y_wait(0)
    x_step(0, 1)
    mid_send(0, 0)
    mid_send(0, 1)
    x_step(1, 0)
    weights_wait()
    z_start()
    x_step(1, 1)
    mid_step(0)
    x_step(2, 0)
    z_step(0, 0)
    x_step(2, 1)
    mid_step(1)
    z_step(0, 1)
    loads[0].wait()
    loads[1].wait()
    y_waits(1, 4)
    gate_up(0)
    x_step(3, 0)
    x_step(3, 1)
    mid_step(2)
    z_step(1, 0)
    y_waits(4, 6)
    gate_up(1)
    z_step(1, 1)
    hidden_step(0, 0)
    mid_step(3)
    y_waits(6, 8)
    gate_up(2)
    z_step(2, 0)
    hidden_step(0, 1)
    hidden_step(1, 0)
    z_step(2, 1)
    hidden_step(2, 0)
    hidden_step(0, 2)
    hidden_step(1, 1)
    z_step(3, 0)
    z_step(3, 1)
    hidden_step(2, 1)
    hidden_step(0, 3)
    hidden_step(1, 2)
    loads[2].wait()
    core_wait()
    hidden_step(2, 2)
    down(0, range(8), True)
    part_send(0)
    hidden_step(1, 3)
    down(1, range(8), True)
    part_send(1)
    down(2, (0, 1, 7, 2, 6, 3, 5), True)
    hidden_step(2, 3)
    down(2, (4,), False)
    part_send(2)

    for lane in (0, 1):
        rows[lane] = part_f[64 * lane : 64 * lane + 16, :]
    for d in (1, 7, 2, 6, 3, 5, 4):
        arrive(arrived.at[d], ps.at[d], pr.at[d])
        rows[...] += arrived[d].astype(jnp.float32)
    for lane in (0, 1):
        for j in range(16):
            outgo[lane, j] = rows[lane, j : j + 1, :]
    own = pltpu.make_async_copy(outgo.at[ylo, reg], final.at[ylo, reg], own_sem)
    own.start()
    for swap in (0, 1):
        lane = 1 - ylo if swap else ylo
        for t in range(16):
            if swap or t:
                push(outgo.at[lane, lax.rem(reg + t, 16)], final.at[ylo, reg],
                     fs.at[swap, t], fr.at[swap, t], regroup_peer(swap, t))
    for copy in sends:
        copy.wait_send()
    own.wait()
    for swap in (0, 1):
        lane = 1 - ylo if swap else ylo
        for t in range(16):
            if swap or t:
                arrive(final.at[lane, lax.rem(reg + 16 - t, 16)], fs.at[swap, t], fr.at[swap, t])
    for lane in (0, 1):
        for g in range(16):
            rows[lane, g : g + 1, :] = final[lane, g]
        out_ref[:, lane * EIGHTH : (lane + 1) * EIGHTH] = rows[lane].astype(jnp.bfloat16)


def on_device(tokens, kinds, slots, gains, gate_weight, up_weight, down_weight):
    vmem = pl.BlockSpec(memory_space=pltpu.VMEM)
    hbm = pl.BlockSpec(memory_space=pl.ANY)
    bf16, f32, dma = jnp.bfloat16, jnp.float32, pltpu.SemaphoreType.DMA
    return pl.pallas_call(
        kernel,
        out_shape=pltpu.VMEM((16, D // 4), bf16),
        in_specs=[hbm] * 7,
        out_specs=vmem,
        scratch_shapes=[
            pltpu.VMEM((16, D), bf16),
            pltpu.VMEM((1, 16), jnp.int32),
            pltpu.VMEM((1, 16), jnp.int32),
            pltpu.VMEM((8, D), f32),
            pltpu.VMEM((2, 8, 16, D), bf16),
            pltpu.VMEM((D, UNITS), bf16),
            pltpu.VMEM((D, UNITS), bf16),
            pltpu.VMEM((8, UNITS, EIGHTH), bf16),
            pltpu.VMEM((8, 256, UNITS), bf16),
            pltpu.VMEM((128, UNITS), f32),
            pltpu.VMEM((128, UNITS), f32),
            pltpu.VMEM((256, EIGHTH), f32),
            pltpu.VMEM((2, 8, 16, EIGHTH), bf16),
            pltpu.VMEM((8, 2, 16, EIGHTH), bf16),
            pltpu.VMEM((2, 16, 1, EIGHTH), f32),
            pltpu.VMEM((2, 16, 1, EIGHTH), f32),
            pltpu.VMEM((2, 16, EIGHTH), f32),
            dma((7,)),
            dma((2, 4, 2)), dma((2, 4, 2)),
            dma((2, 4)), dma((2, 4)),
            dma((8, 2)), dma((8, 2)),
            dma((8,)), dma((8,)),
            dma((2, 4, 2)), dma((2, 4, 2)),
            dma((8, 2)), dma((8, 2)),
            dma((3, 2, 4)), dma((3, 2, 4)),
            dma((8,)), dma((8,)),
            dma((2, 16)), dma((2, 16)),
            dma(()),
        ],
        compiler_params=pltpu.CompilerParams(collective_id=0, has_side_effects=True),
    )(tokens, kinds.reshape(1, 16), slots, gains, gate_weight, up_weight, down_weight)


def solution(mesh):
    placed = (
        P(("blk", "regroup"), None),
        P(("blk", "regroup")),
        P(("blk", "regroup"), None),
        P(),
        P(None, ("blk", "hid")),
        P(None, ("blk", "hid")),
        P(("blk", "hid"), None),
    )
    return jax.shard_map(
        on_device,
        mesh=mesh,
        in_specs=placed,
        out_specs=P(("blk", "regroup"), "hid"),
        check_vma=False,
    )
```

time: 85.5 us -> 78.3 us (0.916)
  Pallas kernels: 83.8 us -> 77.5 us
    pallas_call x1, Pallas kernels: 83.8 us -> 77.5 us  [on_device(): pl.pallas_call(kernel, out_shape=pltpu.VMEM((16, D // 4), bf16), in_specs...]
where the time goes in v2:
time: 78.3 us; the launch traced here: 78.1 us
  Pallas kernels  77.5 us (99%)
    pallas_call x1, Pallas kernels, on_device(): pl.pallas_call(kernel, out_shape=pltpu.VMEM((16, D // 4), bf16), in_specs...  77.5 us

profile of v2, /device:TPU:1, one launch (start us, length us, event | category | flops | bytes accessed | tf_op | source)
XLA Modules:
  0.0 78.1 jit_solution(3751681258934629219)
XLA Ops:
  0.0 77.5 %shard_map.73 = bf16[16,1536]{1,0:T(8,128)(2,1)S(1)} custom-call(bf16[16,6144]{1,0:T(8,128)(2,1)} %tokens_hbm.1, s32[1,16]{1,0:T(1,128)} %bitcast.1, s32[1,16]{1,0:T(1,128)} %slots_hbm.1, f32[8,6144]{1,0:T(8,128)} %gains_hbm.1, bf16[6144,256]{1,0:T(8,128)(2,1)} %gate_hbm.1, bf16[6144,256]{1,0:T(8,128)(2,1)} %up_hbm.1, bf16[256,6144]{1,0:T(8,128)(2,1)} %down_hbm.1), custom_call_target="tpu_custom_call" | custom-call | tf_op jit(solution)/shard_map/pallas_call | solution.py:368
  77.5 0.6 copy.9

commit v3 on v2

--- a/solution.py
+++ b/solution.py
@@ -323,17 +323,17 @@
     hidden_step(2, 2)
     down(0, range(8), True)
     part_send(0)
+    down(2, (0, 1, 7, 2, 6, 3, 5), True)
     hidden_step(1, 3)
-    down(1, range(8), True)
-    part_send(1)
-    down(2, (0, 1, 7, 2, 6, 3, 5), True)
     hidden_step(2, 3)
     down(2, (4,), False)
     part_send(2)
+    down(1, range(8), True)
+    part_send(1)
 
     for lane in (0, 1):
         rows[lane] = part_f[64 * lane : 64 * lane + 16, :]
-    for d in (1, 7, 2, 6, 3, 5, 4):
+    for d in (1, 7, 2, 5, 4, 6, 3):
         arrive(arrived.at[d], ps.at[d], pr.at[d])
         rows[...] += arrived[d].astype(jnp.float32)
     for lane in (0, 1):
@@ -341,12 +341,13 @@
             outgo[lane, j] = rows[lane, j : j + 1, :]
     own = pltpu.make_async_copy(outgo.at[ylo, reg], final.at[ylo, reg], own_sem)
     own.start()
-    for swap in (0, 1):
+    for swap, t in sorted(
+        [(swap, t) for swap in (0, 1) for t in range(16) if swap or t],
+        key=lambda hop: -(2 * hop[0] + min(hop[1], 16 - hop[1])),
+    ):
         lane = 1 - ylo if swap else ylo
-        for t in range(16):
-            if swap or t:
-                push(outgo.at[lane, lax.rem(reg + t, 16)], final.at[ylo, reg],
-                     fs.at[swap, t], fr.at[swap, t], regroup_peer(swap, t))
+        push(outgo.at[lane, lax.rem(reg + t, 16)], final.at[ylo, reg],
+             fs.at[swap, t], fr.at[swap, t], regroup_peer(swap, t))
     for copy in sends:
         copy.wait_send()
     own.wait()

time: 78.3 us -> 78.8 us (level)
  no operation moved by 1% of the time
where the time goes in v3:
time: 78.8 us; the launch traced here: 78.7 us
  Pallas kernels  78 us (99%)
    pallas_call x1, Pallas kernels, on_device(): pl.pallas_call(kernel, out_shape=pltpu.VMEM((16, D // 4), bf16), in_specs...  78 us

profile of v3, /device:TPU:1, one launch (start us, length us, event | category | flops | bytes accessed | tf_op | source)
XLA Modules:
  0.0 78.7 jit_solution(12047483810890263340)
XLA Ops:
  0.0 78.0 %shard_map.73 = bf16[16,1536]{1,0:T(8,128)(2,1)S(1)} custom-call(bf16[16,6144]{1,0:T(8,128)(2,1)} %tokens_hbm.1, s32[1,16]{1,0:T(1,128)} %bitcast.1, s32[1,16]{1,0:T(1,128)} %slots_hbm.1, f32[8,6144]{1,0:T(8,128)} %gains_hbm.1, bf16[6144,256]{1,0:T(8,128)(2,1)} %gate_hbm.1, bf16[6144,256]{1,0:T(8,128)(2,1)} %up_hbm.1, bf16[256,6144]{1,0:T(8,128)(2,1)} %down_hbm.1), custom_call_target="tpu_custom_call" | custom-call | tf_op jit(solution)/shard_map/pallas_call | solution.py:369
  78.0 0.6 copy.9
